TPU v7x, 512 devices: a whole 4x8x8 slice. The times are simulated.
512 devices in a mesh: dp: 16 (over y, core), seq: 32 (over z, x).
Axes of the slice: x: 4, y: 8, z: 8, core: 2. Of those that a mesh axis runs over, the one named last changes fastest.
Arguments:
- hidden: bfloat16 [65536, 2048], P(('dp', 'seq')), may hold values from -6 to 6
- queries: bfloat16 [65536, 2048], P(('dp', 'seq')), may hold values from -360 to 360
- values: bfloat16 [65536, 512], P(('dp', 'seq')), may hold values from -6 to 6
- row_target: int32 [65536], P(('dp', 'seq')), may hold values from 0 to 4095, as said below
- key_weight: bfloat16 [2048, 512], P(('dp', 'seq')), may hold values from -0.125 to 0.125
- dialogue_lengths: int32 [16, 64], P('dp'), may hold values from 1 to 256, 4096 in all within a row
- teacher_pick: int32 [65536, 128], P(('dp', 'seq')), may hold values from 0 to 65279
- teacher_prob: float32 [65536, 128], P(('dp', 'seq')), may hold values from 0.02 to 1
Outputs:
- attn_out: bfloat16 [65536, 2048], P(('dp', 'seq'))
- token_loss: float32 [65536], P(('dp', 'seq'))
- weight_grad: float32 [2048, 512], P(('dp', 'seq'))
Inputs may be any that keep to these rules, and one draw needn't show every extreme that they name: Within each pack, row_target holds every position 0 to 4095 once. Of the 128 rows of one device, at most 6 have targets in one block of 128 positions (target // 128 names the block), and in every draw some device sends exactly 6 to some block.
All inputs are finite; a program needn't handle non-finite values.
Results may differ from a plain program's by a relative error of at most 0.012.
The roundings to bfloat16 on the way count: a program that leaves them out, or rounds other values in their place, can miss the bound.
Values may be sent and summed in bfloat16 or wider, within the bound.
No kernel may reach another device: no remote copies, remote signals or barrier semaphores. Data moves between devices by JAX's collectives and lax.ppermute only.
A program may use at most 64 MiB of HBM per device.

v0:
```python
import jax
import jax.numpy as jnp
from jax import lax
from jax.sharding import PartitionSpec as P

HEAD_DIM = 128
SPAN = 2
negative = -1e30
rope_base = 500000.0


def side_by_side(arrays, axis, split_dim, concat_dim, along):
    ends, at = ([], 0)
    for a in arrays[:-1]:
        at += a.shape[along]
        ends.append(at)
    both = jnp.concatenate(arrays, axis=along)
    return tuple(
        jnp.split(
            lax.all_to_all(both, axis, split_axis=split_dim, concat_axis=concat_dim, tiled=True),
            ends,
            axis=along,
        )
    )


def shifted(shard, axis, by):
    devices = lax.axis_size(axis)
    pairs = [(i, i + by) for i in range(devices) if 0 <= i + by < devices]
    return lax.ppermute(shard, axis, pairs)


def rotate(matrix, positions, direction):
    count = matrix.shape[0]
    split = matrix.reshape(count, -1, HEAD_DIM)
    halfway = HEAD_DIM // 2
    frequency = rope_base ** (-2.0 * jnp.arange(halfway, dtype=jnp.float32) / HEAD_DIM)
    angle = positions.astype(jnp.float32)[:, None] * frequency[None, :]
    cosine = jnp.cos(angle)[:, None, :]
    sine = direction * jnp.sin(angle)[:, None, :]
    first_half = split[..., :halfway]
    second_half = split[..., halfway:]
    joined = jnp.concatenate(
        [first_half * cosine - second_half * sine, second_half * cosine + first_half * sine],
        axis=-1,
    )
    return joined.reshape(count, -1)


def dialogue_starts(lengths, positions):
    ending = jnp.cumsum(lengths)
    picked = jnp.where(ending[None, :] <= positions[:, None], lengths[None, :], 0)
    return jnp.sum(picked, axis=1)


def block_targets(label_index, label_prob, key_start, width):
    within = label_index - key_start
    columns = jnp.arange(width, dtype=jnp.int32)
    matches = within[..., None] == columns[None, None, None, :]
    table = jnp.sum(jnp.where(matches, label_prob[..., None], 0.0), axis=2)
    return jnp.transpose(table, (1, 0, 2))


def project_keys(inputs, key_weight):
    return jnp.dot(
        inputs,
        lax.all_gather(key_weight, ("dp", "seq"), axis=0, tiled=True),
        preferred_element_type=jnp.float32,
    )


def move_rows(first_rows, second_rows, third_rows, row_places):
    return (
        *side_by_side((first_rows, second_rows, third_rows), "seq", 0, 0, 1),
        lax.all_to_all(row_places, "seq", split_axis=0, concat_axis=0, tiled=True),
    )


def guarded(compute, operands):
    return compute(*operands)


def local(
    hidden, queries, values, row_target, key_weight, dialogue_lengths, teacher_pick, teacher_prob
):
    local_rows = hidden.shape[0]
    seq_count = lax.axis_size("seq")
    seq_index = lax.axis_index("seq")
    device_count = seq_count * lax.axis_size("dp")
    capacity = local_rows // seq_count + local_rows // (2 * seq_count)
    head_count = queries.shape[1] // HEAD_DIM
    kv_count = values.shape[1] // HEAD_DIM
    group_size = head_count // kv_count
    top_count = teacher_pick.shape[1] // head_count
    scaling = HEAD_DIM ** (-0.5)
    destination = row_target // local_rows
    offset_in = row_target - destination * local_rows
    one_hot = (destination[:, None] == jnp.arange(seq_count, dtype=jnp.int32)[None, :]).astype(
        jnp.int32
    )
    rank_in = jnp.sum((jnp.cumsum(one_hot, axis=0) - one_hot) * one_hot, axis=1)
    slot_of = destination * capacity + rank_in

    def parcel(data, filler):
        holder = jnp.full((seq_count * capacity,) + data.shape[1:], filler, data.dtype)
        return holder.at[slot_of].set(data)

    def settle(data, places):
        holder = jnp.zeros((local_rows,) + data.shape[1:], data.dtype)
        return holder.at[places].set(data, mode="drop")

    positions = seq_index * local_rows + jnp.arange(local_rows, dtype=jnp.int32)
    received = move_rows(
        parcel(hidden, 0), parcel(queries, 0), parcel(values, 0), parcel(offset_in, local_rows)
    )
    hidden_seq = settle(received[0], received[3])
    queries_seq = settle(received[1], received[3])
    values_seq = settle(received[2], received[3])
    keys_seq = rotate(project_keys(hidden_seq, key_weight), positions, 1.0).astype(jnp.bfloat16)
    starts = dialogue_starts(dialogue_lengths[0], positions)
    reach = (positions - starts + 1)[:, None]
    label_index = (starts[:, None] + teacher_pick % reach).reshape(
        local_rows, head_count, top_count
    )
    label_prob = teacher_prob.reshape(local_rows, head_count, top_count)
    target_mass = jnp.sum(label_prob, axis=2).T.reshape(kv_count, group_size, local_rows)
    entropy = jnp.sum(label_prob * jnp.log(label_prob), axis=(1, 2))
    query_heads = queries_seq.reshape(local_rows, kv_count, group_size, HEAD_DIM)
    earliest = jnp.min(starts)
    blocks = [(keys_seq, values_seq)]
    for distance in range(1, SPAN + 1):
        blocks.append(shifted((keys_seq, values_seq), "seq", distance))

    def scores_of(key_block, key_start):
        key_heads = key_block.reshape(local_rows, kv_count, HEAD_DIM)
        score = (
            jnp.einsum("tkgd,wkd->kgtw", query_heads, key_heads, preferred_element_type=jnp.float32)
            * scaling
        )
        key_pos = key_start + jnp.arange(local_rows, dtype=jnp.int32)
        allowed = (key_pos[None, :] >= starts[:, None]) & (key_pos[None, :] <= positions[:, None])
        held = jnp.where(allowed[None, None], score, negative)
        table = block_targets(label_index, label_prob, key_start, local_rows)
        return (score, held, table.reshape(kv_count, group_size, local_rows, local_rows))

    def first_pass(key_block, key_start):
        score, held, table = scores_of(key_block, key_start)
        block_top = jnp.max(held, axis=-1)
        block_total = jnp.sum(jnp.exp(held - block_top[..., None]), axis=-1)
        return (block_top, block_total, jnp.sum(table * score, axis=-1))

    tops, totals, pickings, alive_list = ([], [], [], [])
    for distance, (key_block, value_block) in enumerate(blocks):
        key_start = (seq_index - distance) * local_rows
        alive = earliest < key_start + local_rows
        alive_list.append((alive, key_start))
        block_top, block_total, picking = guarded(first_pass, (key_block, key_start))
        tops.append(block_top)
        totals.append(block_total)
        pickings.append(picking)
    top_all = jnp.max(jnp.stack(tops), axis=0)
    total_all = jnp.sum(jnp.stack(totals) * jnp.exp(jnp.stack(tops) - top_all[None]), axis=0)
    lse = top_all + jnp.log(total_all)
    picked_all = jnp.sum(jnp.stack(pickings), axis=0)
    token_loss = (
        entropy - jnp.sum(picked_all, axis=(0, 1)) + jnp.sum(target_mass * lse, axis=(0, 1))
    ) / head_count

    def second_pass(key_block, value_block, key_start):
        score, held, table = scores_of(key_block, key_start)
        weight = jnp.exp(held - lse[..., None])
        value_heads = value_block.reshape(local_rows, kv_count, HEAD_DIM)
        partial_value = jnp.einsum(
            "kgtw,wkd->tkgd",
            weight.astype(jnp.bfloat16),
            value_heads,
            preferred_element_type=jnp.float32,
        )
        slope = ((weight * target_mass[..., None] - table) / head_count).astype(jnp.bfloat16)
        gradient = (
            jnp.einsum("kgtw,tkgd->wkd", slope, query_heads, preferred_element_type=jnp.float32)
            * scaling
        )
        return (partial_value, gradient.reshape(local_rows, kv_count * HEAD_DIM))

    output_sum = jnp.zeros((local_rows, kv_count, group_size, HEAD_DIM), jnp.float32)
    block_grads = []
    for distance, (key_block, value_block) in enumerate(blocks):
        alive, key_start = alive_list[distance]
        partial_value, gradient = guarded(second_pass, (key_block, value_block, key_start))
        output_sum = output_sum + partial_value
        block_grads.append(gradient)
    attn_out = output_sum.astype(jnp.bfloat16).reshape(local_rows, head_count * HEAD_DIM)
    rotated_grad = block_grads[0]
    for distance in range(1, SPAN + 1):
        rotated_grad = rotated_grad + shifted(
            block_grads[distance].astype(jnp.bfloat16), "seq", -distance
        ).astype(jnp.float32)
    key_grad = rotate(rotated_grad, positions, -1.0).astype(jnp.bfloat16)
    inverse_root = (local_rows * device_count) ** (-0.5)
    weight_grad = lax.psum_scatter(
        jnp.einsum("td,tc->dc", hidden_seq, key_grad, preferred_element_type=jnp.float32)
        * inverse_root,
        ("dp", "seq"),
        scatter_dimension=0,
        tiled=True,
    )
    return (attn_out, token_loss, weight_grad)


def solution(mesh):
    placed = (
        P(("dp", "seq"), None),
        P(("dp", "seq"), None),
        P(("dp", "seq"), None),
        P(("dp", "seq")),
        P(("dp", "seq"), None),
        P("dp", None),
        P(("dp", "seq"), None),
        P(("dp", "seq"), None),
    )
    return jax.shard_map(
        local,
        mesh=mesh,
        in_specs=placed,
        out_specs=(P(("dp", "seq"), None), P(("dp", "seq")), P(("dp", "seq"), None)),
        check_vma=False,
    )
```

profile of v0, /device:TPU:24, one launch (start us, length us, event | category | flops | bytes accessed | tf_op | source)
XLA Modules:
  0.0 468.3 jit_solution(1909932500916336995)
XLA Ops:
  10.7 13.2 %all-to-all-start = ((s32[32,6,1]{1,2,0:T(1,128)}), s32[32,6,1]{1,2,0:T(1,128)S(1)}, u32[]{:S(2)}, u32[]{:S(2)}) async-start(s32[32,6,1]{1,2,0:T(1,128)} %bitcast), calls=%async_computation | async-start | bytes 32768 | tf_op jit(solution)/shard_map/all_to_all | solution.py:75
  23.9 1.5 scatter_custom_fusion.3
  25.4 2.1 scatter_custom_fusion.2
  27.5 2.1 scatter_custom_fusion.1
  29.8 1.7 all_to_all.19
  31.5 2.1 all-to-all-done
  33.6 7.8 %all-to-all-start.1 = ((bf16[32,6,4608]{2,1,0:T(8,128)(2,1)}), bf16[32,6,4608]{2,1,0:T(8,128)(2,1)S(1)}, u32[]{:S(2)}, u32[]{:S(2)}) async-start(bf16[32,6,4608]{2,1,0:T(8,128)(2,1)} %all_to_all.19), calls=%async_computation.1 | async-start | bytes 4718592 | tf_op jit(solution)/shard_map/all_to_all | solution.py:20
  44.4 1.4 copy.109
  45.8 2.2 copy.113
  48.1 2.2 copy.107
  50.3 13.4 %select_reduce_fusion.1 = (f32[128,16,128]{2,1,0:T(8,128)}, f32[128,16,128]{2,1,0:T(8,128)}, f32[128,16,128]{2,1,0:T(8,128)}) fusion(s32[128,16,8]{2,1,0:T(8,128)S(1)} %copy.111, f32[128,16,8]{2,1,0:T(8,128)} %copy.109, s32[128,16,8]{2,1,0:T(8,128)} %copy.113, s32[128,16,8]{2,1,0:T(8,128)} %copy.107), kind=kLoop, calls=%fused_computation.9 | loop fusion | flops 18087936 | bytes 3407872 | tf_op jit(solution)/shard_map/reduce_sum | solution.py:60
  63.6 2.6 copy.114
  66.3 2.6 copy.112
  68.8 1.4 copy.110
  72.8 25.2 %all-to-all-done.1 = bf16[32,6,4608]{2,1,0:T(8,128)(2,1)S(1)} async-done(((bf16[32,6,4608]{2,1,0:T(8,128)(2,1)}), bf16[32,6,4608]{2,1,0:T(8,128)(2,1)S(1)}, u32[]{:S(2)}, u32[]{:S(2)}) %all-to-all-start.1) | async-done | bytes 1769504 | tf_op jit(solution)/shard_map/all_to_all | solution.py:20
  98.0 1.6 all_to_all.21
  99.6 2.6 scatter_custom_fusion.6
  102.2 2.4 scatter_custom_fusion.5
  104.9 31.5 %all-gather.3.cloned.1.call-done = bf16[512,4,512]{2,1,0:T(4,128)(2,1)} async-done(((bf16[1,4,512]{2,1,0:T(4,128)(2,1)}), bf16[512,4,512]{2,1,0:T(4,128)(2,1)}) %all-gather.3.cloned.1.call-update) | async-done | bytes 2097168 | tf_op jit(solution)/shard_map/all_gather | solution.py:67
  136.5 4.0 reshape.528
  140.4 2.1 fusion.77
  143.2 4.5 collective-permute-start.1
  147.7 2.7 collective-permute-start
  151.7 2.0 collective-permute-done
  159.4 6.5 %collective-permute-done.5 = bf16[128,512]{0,1:T(8,128)(2,1)S(1)} collective-permute-done((bf16[128,512]{0,1:T(8,128)(2,1)S(1)}, bf16[128,512]{0,1:T(8,128)(2,1)S(1)}, u32[]{:S(2)}, u32[]{:S(2)}) %collective-permute-start.5) | collective-permute-done | bytes 131104 | tf_op jit(solution)/shard_map/ppermute | solution.py:30
  165.9 2.1 collective-permute-done.4
  168.7 2.7 convolution_multiply_fusion
  171.4 1.8 scatter_custom_fusion.4
  173.2 4.5 collective-permute-start.2
  177.7 6.0 %collective-permute-start.3 = (bf16[128,512]{1,0:T(8,128)(2,1)S(1)}, bf16[128,512]{1,0:T(8,128)(2,1)}, u32[]{:S(2)}, u32[]{:S(2)}) collective-permute-start(bf16[128,512]{1,0:T(8,128)(2,1)S(1)} %scatter_custom_fusion.4), channel_id=1, source_target_pairs={{0,2},{1,3},{2,4},{3,5},{4,6},{5,7},{6,8},{7,9},{8,10},{9,11},{10,... | collective-permute-start | bytes 393224 | tf_op jit(solution)/shard_map/ppermute | solution.py:30
  184.4 1.7 copy.102
  190.7 269.5 %all-reduce.3.cloned.1.call-done = f32[2048,512]{1,0:T(8,128)} async-done(((f32[2048,512]{1,0:T(8,128)}), f32[2048,512]{1,0:T(8,128)}) %all-reduce.3.cloned.1.call-update) | async-done | bytes 4194320
  (108 shorter events, 24.1 us)
Async XLA Ops:
  7.2 129.3 %all-gather.3.cloned.1.call-start = ((), (), s32[]{:S(2)}) async-start(), calls=%async_computation.2 | async-start | bytes 2101248 | tf_op jit(solution)/shard_map/all_gather | solution.py:67
  10.7 22.9 %all-to-all-start = ((s32[32,6,1]{1,2,0:T(1,128)}), s32[32,6,1]{1,2,0:T(1,128)S(1)}, u32[]{:S(2)}, u32[]{:S(2)}) async-start(s32[32,6,1]{1,2,0:T(1,128)} %bitcast), calls=%async_computation | async-start | bytes 32768 | tf_op jit(solution)/shard_map/all_to_all | solution.py:75
  29.7 12.2 %copy-start.15 = (s32[1,64]{1,0:T(1,128)S(1)}, s32[1,64]{1,0:T(1,128)}, u32[]{:S(2)}) copy-start(s32[1,64]{1,0:T(1,128)} %param.13) | copy-start | bytes 772
  29.8 12.5 %copy-start.9 = (s32[128,128]{1,0:T(8,128)S(1)}, s32[128,128]{1,0:T(8,128)}, u32[]{:S(2)}) copy-start(s32[128,128]{1,0:T(8,128)} %param.14) | copy-start | bytes 196612
  31.5 12.8 %copy-start.7 = (f32[128,128]{1,0:T(8,128)S(1)}, f32[128,128]{1,0:T(8,128)}, u32[]{:S(2)}) copy-start(f32[128,128]{1,0:T(8,128)} %param.15) | copy-start | bytes 196612
  33.6 64.4 %all-to-all-start.1 = ((bf16[32,6,4608]{2,1,0:T(8,128)(2,1)}), bf16[32,6,4608]{2,1,0:T(8,128)(2,1)S(1)}, u32[]{:S(2)}, u32[]{:S(2)}) async-start(bf16[32,6,4608]{2,1,0:T(8,128)(2,1)} %all_to_all.19), calls=%async_computation.1 | async-start | bytes 4718592 | tf_op jit(solution)/shard_map/all_to_all | solution.py:20
  41.4 418.7 %all-reduce.3.cloned.1.call-start = ((), (), s32[]{:S(2)}) async-start(), calls=%async_computation.3 | async-start | bytes 8388608
  42.0 1.9 copy-start.13
  42.5 1.3 copy-start.11
  63.6 5.2 %copy-start.6 = (f32[128,16,128]{2,1,0:T(8,128)S(1)}, f32[128,16,128]{2,1,0:T(8,128)}, u32[]{:S(2)}) copy-start(f32[128,16,128]{2,1,0:T(8,128)} %get-tuple-element.19) | copy-start | bytes 3145732
  63.6 6.7 %copy-start.12 = (s32[128]{0:T(128)S(1)}, s32[128]{0:T(128)}, u32[]{:S(2)}) copy-start(s32[128]{0:T(128)} %copy-done.11) | copy-start | bytes 1540
  63.6 6.7 %copy-start.14 = (s32[128]{0:T(128)S(1)}, s32[128]{0:T(128)}, u32[]{:S(2)}) copy-start(s32[128]{0:T(128)} %copy-done.13) | copy-start | bytes 1540
  72.8 32.2 %copy-start.17 = (s32[192,1]{0,1:T(1,128)}, s32[192,1]{0,1:T(1,128)S(1)}, u32[]{:S(2)}) copy-start(s32[192,1]{0,1:T(1,128)S(1)} %compare_select_fusion) | copy-start | bytes 2308
  140.4 10.3 %copy-start.4 = (f32[16,128,128]{1,2,0:T(8,128)S(1)}, f32[16,128,128]{1,2,0:T(8,128)}, u32[]{:S(2)}) copy-start(f32[16,128,128]{1,2,0:T(8,128)} %copy.110) | copy-start | bytes 3145732
  143.2 8.1 %collective-permute-start.1 = (bf16[128,512]{0,1:T(8,128)(2,1)S(1)}, bf16[128,512]{0,1:T(8,128)(2,1)S(1)}, u32[]{:S(2)}, u32[]{:S(2)}) collective-permute-start(bf16[128,512]{0,1:T(8,128)(2,1)S(1)} %bitcast.171), channel_id=1, source_target_pairs={{0,2},{1,3},{2,4},{3,5},{4,6},{5,7},{6,8},{7,9},{8,10},{9,11},{10,... | collective-permute-start | bytes 393224 | tf_op jit(solution)/shard_map/ppermute | solution.py:30
  147.7 5.9 %collective-permute-start = (bf16[128,512]{0,1:T(8,128)(2,1)S(1)}, bf16[128,512]{0,1:T(8,128)(2,1)S(1)}, u32[]{:S(2)}, u32[]{:S(2)}) collective-permute-start(bf16[128,512]{0,1:T(8,128)(2,1)S(1)} %bitcast.172), channel_id=1, source_target_pairs={{0,1},{1,2},{2,3},{3,4},{4,5},{5,6},{6,7},{7,8},{8,9},{9,10},{10,1... | collective-permute-start | bytes 393224 | tf_op jit(solution)/shard_map/ppermute | solution.py:30
  150.4 3.6 copy-start.2
  150.7 8.2 %copy-start = (f32[4,4,128,128]{2,3,1,0:T(8,128)}, f32[4,4,128,128]{2,3,1,0:T(8,128)S(1)}, u32[]{:S(2)}) copy-start(f32[4,4,128,128]{2,3,1,0:T(8,128)S(1)} %get-tuple-element.48) | copy-start | bytes 3145732
  150.8 3.6 copy-start.3
  154.4 4.5 copy-start.5
  156.3 9.6 %collective-permute-start.5 = (bf16[128,512]{0,1:T(8,128)(2,1)S(1)}, bf16[128,512]{0,1:T(8,128)(2,1)S(1)}, u32[]{:S(2)}, u32[]{:S(2)}) collective-permute-start(bf16[128,512]{0,1:T(8,128)(2,1)S(1)} %bitcast.170), channel_id=1, source_target_pairs={{2,0},{3,1},{4,2},{5,3},{6,4},{7,5},{8,6},{9,7},{10,8},{11,9},{12,... | collective-permute-start | bytes 393224 | tf_op jit(solution)/shard_map/ppermute | solution.py:30
  157.6 10.4 %collective-permute-start.4 = (bf16[128,512]{0,1:T(8,128)(2,1)S(1)}, bf16[128,512]{0,1:T(8,128)(2,1)S(1)}, u32[]{:S(2)}, u32[]{:S(2)}) collective-permute-start(bf16[128,512]{0,1:T(8,128)(2,1)S(1)} %bitcast.169), channel_id=1, source_target_pairs={{1,0},{2,1},{3,2},{4,3},{5,4},{6,5},{7,6},{8,7},{9,8},{10,9},{11,1... | collective-permute-start | bytes 393224 | tf_op jit(solution)/shard_map/ppermute | solution.py:30
  168.6 15.0 %copy-start.8 = (f32[128,128]{1,0:T(8,128)S(1)}, f32[128,128]{1,0:T(8,128)}, u32[]{:S(2)}) copy-start(f32[128,128]{1,0:T(8,128)} %param.15) | copy-start | bytes 196612
  171.4 15.8 %copy-start.1 = (f32[4,4,128,128]{2,3,1,0:T(8,128)S(1)}, f32[4,4,128,128]{2,3,1,0:T(8,128)}, u32[]{:S(2)}) copy-start(f32[4,4,128,128]{2,3,1,0:T(8,128)} %copy-done) | copy-start | bytes 3145732
  173.2 11.2 %collective-permute-start.2 = (bf16[128,512]{1,0:T(8,128)(2,1)S(1)}, bf16[128,512]{1,0:T(8,128)(2,1)}, u32[]{:S(2)}, u32[]{:S(2)}) collective-permute-start(bf16[128,512]{1,0:T(8,128)(2,1)S(1)} %scatter_custom_fusion.4), channel_id=1, source_target_pairs={{0,1},{1,2},{2,3},{3,4},{4,5},{5,6},{6,7},{7,8},{8,9},{9,10},{10,1... | collective-permute-start | bytes 393224 | tf_op jit(solution)/shard_map/ppermute | solution.py:30
  177.7 8.4 %collective-permute-start.3 = (bf16[128,512]{1,0:T(8,128)(2,1)S(1)}, bf16[128,512]{1,0:T(8,128)(2,1)}, u32[]{:S(2)}, u32[]{:S(2)}) collective-permute-start(bf16[128,512]{1,0:T(8,128)(2,1)S(1)} %scatter_custom_fusion.4), channel_id=1, source_target_pairs={{0,2},{1,3},{2,4},{3,5},{4,6},{5,7},{6,8},{7,9},{8,10},{9,11},{10,... | collective-permute-start | bytes 393224 | tf_op jit(solution)/shard_map/ppermute | solution.py:30
  187.5 2.7 copy-start.10
  187.5 2.7 copy-start.16
Sparse Core Ops, SparseCore 0:
  12.2 124.2 all-gather.2
  171.5 288.5 all-reduce.2
where the time goes:
time: 469 us; the launch traced here: 468 us
  waiting for transfers between devices  340 us (72%)
  local copies, waits for them, and re-layouts  41.6 us (9%)
  starting transfers between devices  41.3 us (9%)
  other arithmetic  21.7 us (5%)
  between operations  14.6 us (3%)
  matrix products  9.27 us (2%)
    unnamed x3, waiting for transfers between devices  270 us
    all_gather x1, waiting for transfers between devices, project_keys(): lax.all_gather(key_weight, ('dp', 'seq'), axis=0, tiled=True)  31.5 us
    all_to_all x1, waiting for transfers between devices, side_by_side(): lax.all_to_all(both, axis, split_axis=split_dim, concat_axis=concat_dim,...  25.2 us
    ppermute x6, starting transfers between devices, shifted(): return lax.ppermute(shard, axis, pairs)  20.3 us
    reduce_sum x1, other arithmetic, block_targets(): table = jnp.sum(jnp.where(matches, label_prob[..., None], 0.0), axis=2)  13.4 us
    all_to_all x1, starting transfers between devices, move_rows(): lax.all_to_all(row_places, 'seq', split_axis=0, concat_axis=0, tiled=True)  13.2 us
    ppermute x6, waiting for transfers between devices, shifted(): return lax.ppermute(shard, axis, pairs)  10.8 us
  transfers between devices with their start and end apart: 10, of which 8 were waited for; matrix products, arithmetic and copies ran while one was open for 12% of the time, Pallas kernels for 0%

commit v1 on v0

--- a/solution.py
+++ b/solution.py
@@ -64,7 +64,15 @@
 def project_keys(inputs, key_weight):
     return jnp.dot(
         inputs,
-        lax.all_gather(key_weight, ("dp", "seq"), axis=0, tiled=True),
+        jnp.concatenate(
+            lax.all_to_all(
+                jnp.stack(lax.axis_size(("dp", "seq")) * [key_weight], axis=0),
+                concat_axis=0,
+                axis_name=("dp", "seq"),
+                split_axis=0,
+            ),
+            axis=0,
+        ),
         preferred_element_type=jnp.float32,
     )
 

time: 469 us -> 496 us (1.058)
  blocking collectives: 0 us -> 65 us
  waiting for transfers between devices: 340 us -> 292 us
  starting transfers between devices: 41.3 us -> 46.9 us
    all_to_all x0 -> x1, blocking collectives: none -> 65 us  [side_by_side(): lax.all_to_all(both, axis, split_axis=split_dim, concat_axis=concat_dim,...]
    all_gather x1 -> x0, waiting for transfers between devices: 31.5 us -> none  [project_keys(): lax.all_gather(key_weight, ('dp', 'seq'), axis=0, tiled=True)]
    all_to_all x1, waiting for transfers between devices: 25.2 us -> 11.9 us  [project_keys(): lax.all_to_all(jnp.stack(lax.axis_size(('dp', 'seq')) * [key_weight], axi...]
    all_to_all x1, starting transfers between devices: 7.84 us -> 13.8 us  [project_keys(): lax.all_to_all(jnp.stack(lax.axis_size(('dp', 'seq')) * [key_weight], axi...]
    unnamed x3 -> x2, waiting for transfers between devices: 270 us -> 268 us
  transfers between devices with their start and end apart: 10 -> 9, of which waited for: 8 -> 7; matrix products, arithmetic and copies ran while one was open for 12% -> 11% of each run, Pallas kernels for 0% -> 0%
where the time goes in v1:
time: 496 us; the launch traced here: 495 us
  waiting for transfers between devices  292 us (59%)
  blocking collectives  65 us (13%)
  starting transfers between devices  46.9 us (9%)
  local copies, waits for them, and re-layouts  43.7 us (9%)
  other arithmetic  23.2 us (5%)
  between operations  14.6 us (3%)
  matrix products  10.1 us (2%)
    unnamed x2, waiting for transfers between devices  268 us
    all_to_all x1, blocking collectives, side_by_side(): lax.all_to_all(both, axis, split_axis=split_dim, concat_axis=concat_dim,...  65 us
    ppermute x6, starting transfers between devices, shifted(): return lax.ppermute(shard, axis, pairs)  19.6 us
    all_to_all x1, starting transfers between devices, project_keys(): lax.all_to_all(jnp.stack(lax.axis_size(('dp', 'seq')) * [key_weight], axi...  13.8 us
    reduce_sum x1, other arithmetic, block_targets(): table = jnp.sum(jnp.where(matches, label_prob[..., None], 0.0), axis=2)  13.3 us
    all_to_all x1, starting transfers between devices, move_rows(): lax.all_to_all(row_places, 'seq', split_axis=0, concat_axis=0, tiled=True)  13.2 us
    all_to_all x1, waiting for transfers between devices, project_keys(): lax.all_to_all(jnp.stack(lax.axis_size(('dp', 'seq')) * [key_weight], axi...  11.9 us
  transfers between devices with their start and end apart: 9, of which 7 were waited for; matrix products, arithmetic and copies ran while one was open for 11% of the time, Pallas kernels for 0%

profile of v1, /device:TPU:24, one launch (start us, length us, event | category | flops | bytes accessed | tf_op | source)
XLA Modules:
  0.0 495.1 jit_solution(15089956168966462097)
XLA Ops:
  10.0 13.2 %all-to-all-start = ((s32[32,6,1]{1,2,0:T(1,128)}), s32[32,6,1]{1,2,0:T(1,128)S(1)}, u32[]{:S(2)}, u32[]{:S(2)}) async-start(s32[32,6,1]{1,2,0:T(1,128)} %bitcast), calls=%async_computation | async-start | bytes 32768 | tf_op jit(solution)/shard_map/all_to_all | solution.py:83
  23.2 1.5 scatter_custom_fusion.3
  24.6 2.1 scatter_custom_fusion.2
  26.8 2.1 scatter_custom_fusion.1
  29.0 1.7 all_to_all.22
  30.7 2.1 all-to-all-done
  32.8 65.0 %all_to_all.29 = bf16[32,6,4608]{2,1,0:T(8,128)(2,1)S(1)} all-to-all(bf16[32,6,4608]{2,1,0:T(8,128)(2,1)} %all_to_all.22), channel_id=1, replica_groups=mesh['dp'=16,'seq'=32] {'seq'}, dimensions={0} | all-to-all | bytes 3538944 | tf_op jit(solution)/shard_map/all_to_all | solution.py:20
  97.8 1.8 stack.18
  99.7 13.8 %all-to-all-start.2 = ((bf16[512,4,512]{2,1,0:T(4,128)(2,1)}), bf16[512,4,512]{2,1,0:T(4,128)(2,1)}, u32[]{:S(2)}, u32[]{:S(2)}) async-start(bf16[512,4,512]{2,1,0:T(4,128)(2,1)} %stack.18), calls=%async_computation.2 | async-start | bytes 4194304 | tf_op jit(solution)/shard_map/all_to_all | solution.py:68
  117.6 2.2 copy.100
  119.8 2.2 copy.102
  123.4 13.3 %select_reduce_fusion.1 = (f32[128,16,128]{2,1,0:T(8,128)}, f32[128,16,128]{2,1,0:T(8,128)}, f32[128,16,128]{2,1,0:T(8,128)}) fusion(s32[128,16,8]{2,1,0:T(8,128)} %copy.100, f32[128,16,8]{2,1,0:T(8,128)} %copy.98, s32[128,16,8]{2,1,0:T(8,128)} %copy.102, s32[128,16,8]{2,1,0:T(8,128)S(1)} %copy.96), kind=kLoop, calls=%fused_computation.9 | loop fusion | flops 18087936 | bytes 3407872 | tf_op jit(solution)/shard_map/reduce_sum | solution.py:60
  136.8 2.7 copy.101
  139.5 2.6 copy.103
  142.0 1.4 copy.99
  145.0 1.4 reduce.12
  146.5 1.6 all_to_all.24
  148.1 2.4 scatter_custom_fusion.5
  150.6 2.4 scatter_custom_fusion.6
  153.3 11.9 %all-to-all-done.2 = bf16[512,4,512]{2,1,0:T(4,128)(2,1)} async-done(((bf16[512,4,512]{2,1,0:T(4,128)(2,1)}), bf16[512,4,512]{2,1,0:T(4,128)(2,1)}, u32[]{:S(2)}, u32[]{:S(2)}) %all-to-all-start.2) | async-done | bytes 2097184 | tf_op jit(solution)/shard_map/all_to_all | solution.py:68
  165.2 2.5 reshape.459
  167.8 2.5 copy.81
  170.3 2.4 fusion.20
  172.7 2.2 collective-permute-start.1
  174.9 3.7 collective-permute-start
  187.7 4.2 collective-permute-done.4
  191.9 4.1 collective-permute-done.5
  196.1 2.7 convolution_multiply_fusion
  198.8 1.8 scatter_custom_fusion.4
  200.6 7.3 %collective-permute-start.3 = (bf16[128,512]{1,0:T(8,128)(2,1)S(1)}, bf16[128,512]{1,0:T(8,128)(2,1)}, u32[]{:S(2)}, u32[]{:S(2)}) collective-permute-start(bf16[128,512]{1,0:T(8,128)(2,1)S(1)} %scatter_custom_fusion.4), channel_id=1, source_target_pairs={{0,2},{1,3},{2,4},{3,5},{4,6},{5,7},{6,8},{7,9},{8,10},{9,11},{10,... | collective-permute-start | bytes 393224 | tf_op jit(solution)/shard_map/ppermute | solution.py:30
  207.8 3.9 collective-permute-start.2
  218.7 268.2 %all-reduce.3.cloned.1.call-done = f32[2048,512]{1,0:T(8,128)} async-done(((f32[2048,512]{1,0:T(8,128)}), f32[2048,512]{1,0:T(8,128)}) %all-reduce.3.cloned.1.call-update) | async-done | bytes 4194320
  (103 shorter events, 27.4 us)
Async XLA Ops:
  10.0 22.9 %all-to-all-start = ((s32[32,6,1]{1,2,0:T(1,128)}), s32[32,6,1]{1,2,0:T(1,128)S(1)}, u32[]{:S(2)}, u32[]{:S(2)}) async-start(s32[32,6,1]{1,2,0:T(1,128)} %bitcast), calls=%async_computation | async-start | bytes 32768 | tf_op jit(solution)/shard_map/all_to_all | solution.py:83
  30.7 67.1 %copy-start.16 = (bf16[4,512]{1,0:T(4,128)(2,1)S(1)}, bf16[4,512]{1,0:T(4,128)(2,1)}, u32[]{:S(2)}) copy-start(bf16[4,512]{1,0:T(4,128)(2,1)} %param.12) | copy-start | bytes 12292
  32.8 66.8 %copy-start.12 = (s32[32,6,1]{1,2,0:T(1,128)}, s32[32,6,1]{1,2,0:T(1,128)S(1)}, u32[]{:S(2)}) copy-start(s32[32,6,1]{1,2,0:T(1,128)S(1)} %all-to-all-done) | copy-start | bytes 2308
  99.7 14.1 %copy-start.17 = (s32[1,64]{1,0:T(1,128)S(1)}, s32[1,64]{1,0:T(1,128)}, u32[]{:S(2)}) copy-start(s32[1,64]{1,0:T(1,128)} %param.13) | copy-start | bytes 772
  99.7 14.4 %copy-start.10 = (f32[128,128]{1,0:T(8,128)S(1)}, f32[128,128]{1,0:T(8,128)}, u32[]{:S(2)}) copy-start(f32[128,128]{1,0:T(8,128)} %param.15) | copy-start | bytes 196612
  99.7 14.5 %copy-start.11 = (s32[128,128]{1,0:T(8,128)S(1)}, s32[128,128]{1,0:T(8,128)}, u32[]{:S(2)}) copy-start(s32[128,128]{1,0:T(8,128)} %param.14) | copy-start | bytes 196612
  99.7 65.5 %all-to-all-start.2 = ((bf16[512,4,512]{2,1,0:T(4,128)(2,1)}), bf16[512,4,512]{2,1,0:T(4,128)(2,1)}, u32[]{:S(2)}, u32[]{:S(2)}) async-start(bf16[512,4,512]{2,1,0:T(4,128)(2,1)} %stack.18), calls=%async_computation.2 | async-start | bytes 4194304 | tf_op jit(solution)/shard_map/all_to_all | solution.py:68
  113.5 373.4 %all-reduce.3.cloned.1.call-start = ((), (), s32[]{:S(2)}) async-start(), calls=%async_computation.3 | async-start | bytes 8388608
  136.8 5.2 %copy-start.5 = (f32[128,16,128]{2,1,0:T(8,128)S(1)}, f32[128,16,128]{2,1,0:T(8,128)}, u32[]{:S(2)}) copy-start(f32[128,16,128]{2,1,0:T(8,128)} %get-tuple-element.19) | copy-start | bytes 3145732
  143.6 39.9 %copy-start.8 = (pred[128,128]{0,1:T(8,128)(4,1)}, pred[128,128]{0,1:T(8,128)(4,1)S(1)}, u32[]{:S(2)}) copy-start(pred[128,128]{0,1:T(8,128)(4,1)S(1)} %get-tuple-element.38) | copy-start | bytes 49156
  143.6 40.4 %copy-start.6 = (pred[128,128]{0,1:T(8,128)(4,1)}, pred[128,128]{0,1:T(8,128)(4,1)S(1)}, u32[]{:S(2)}) copy-start(pred[128,128]{0,1:T(8,128)(4,1)S(1)} %get-tuple-element.39) | copy-start | bytes 49156
  143.6 43.5 %copy-start.9 = (pred[128,128]{0,1:T(8,128)(4,1)}, pred[128,128]{0,1:T(8,128)(4,1)S(1)}, u32[]{:S(2)}) copy-start(pred[128,128]{0,1:T(8,128)(4,1)S(1)} %get-tuple-element.40) | copy-start | bytes 49156
  170.3 8.8 %copy-start.4 = (f32[16,128,128]{1,2,0:T(8,128)S(1)}, f32[16,128,128]{1,2,0:T(8,128)}, u32[]{:S(2)}) copy-start(f32[16,128,128]{1,2,0:T(8,128)} %copy.99) | copy-start | bytes 3145732
  172.7 8.6 %collective-permute-start.1 = (bf16[128,512]{0,1:T(8,128)(2,1)S(1)}, bf16[128,512]{0,1:T(8,128)(2,1)S(1)}, u32[]{:S(2)}, u32[]{:S(2)}) collective-permute-start(bf16[128,512]{0,1:T(8,128)(2,1)S(1)} %bitcast.183), channel_id=1, source_target_pairs={{0,2},{1,3},{2,4},{3,5},{4,6},{5,7},{6,8},{7,9},{8,10},{9,11},{10,... | collective-permute-start | bytes 393224 | tf_op jit(solution)/shard_map/ppermute | solution.py:30
  174.9 6.0 %collective-permute-start = (bf16[128,512]{0,1:T(8,128)(2,1)S(1)}, bf16[128,512]{0,1:T(8,128)(2,1)S(1)}, u32[]{:S(2)}, u32[]{:S(2)}) collective-permute-start(bf16[128,512]{0,1:T(8,128)(2,1)S(1)} %bitcast.184), channel_id=1, source_target_pairs={{0,1},{1,2},{2,3},{3,4},{4,5},{5,6},{6,7},{7,8},{8,9},{9,10},{10,1... | collective-permute-start | bytes 393224 | tf_op jit(solution)/shard_map/ppermute | solution.py:30
  179.1 8.1 %copy-start = (f32[4,4,128,128]{2,3,1,0:T(8,128)}, f32[4,4,128,128]{2,3,1,0:T(8,128)S(1)}, u32[]{:S(2)}) copy-start(f32[4,4,128,128]{2,3,1,0:T(8,128)S(1)} %get-tuple-element.44) | copy-start | bytes 3145732
  179.1 2.7 copy-start.2
  181.3 1.3 copy-start.3
  184.6 7.3 %collective-permute-start.4 = (bf16[128,512]{0,1:T(8,128)(2,1)S(1)}, bf16[128,512]{0,1:T(8,128)(2,1)S(1)}, u32[]{:S(2)}, u32[]{:S(2)}) collective-permute-start(bf16[128,512]{0,1:T(8,128)(2,1)S(1)} %bitcast.182), channel_id=1, source_target_pairs={{1,0},{2,1},{3,2},{4,3},{5,4},{6,5},{7,6},{8,7},{9,8},{10,9},{11,1... | collective-permute-start | bytes 393224 | tf_op jit(solution)/shard_map/ppermute | solution.py:30
  185.9 10.1 %collective-permute-start.5 = (bf16[128,512]{0,1:T(8,128)(2,1)S(1)}, bf16[128,512]{0,1:T(8,128)(2,1)S(1)}, u32[]{:S(2)}, u32[]{:S(2)}) collective-permute-start(bf16[128,512]{0,1:T(8,128)(2,1)S(1)} %bitcast.181), channel_id=1, source_target_pairs={{2,0},{3,1},{4,2},{5,3},{6,4},{7,5},{8,6},{9,7},{10,8},{11,9},{12,... | collective-permute-start | bytes 393224 | tf_op jit(solution)/shard_map/ppermute | solution.py:30
  198.8 15.8 %copy-start.1 = (f32[4,4,128,128]{2,3,1,0:T(8,128)S(1)}, f32[4,4,128,128]{2,3,1,0:T(8,128)}, u32[]{:S(2)}) copy-start(f32[4,4,128,128]{2,3,1,0:T(8,128)} %copy-done) | copy-start | bytes 3145732
  200.6 11.9 %collective-permute-start.3 = (bf16[128,512]{1,0:T(8,128)(2,1)S(1)}, bf16[128,512]{1,0:T(8,128)(2,1)}, u32[]{:S(2)}, u32[]{:S(2)}) collective-permute-start(bf16[128,512]{1,0:T(8,128)(2,1)S(1)} %scatter_custom_fusion.4), channel_id=1, source_target_pairs={{0,2},{1,3},{2,4},{3,5},{4,6},{5,7},{6,8},{7,9},{8,10},{9,11},{10,... | collective-permute-start | bytes 393224 | tf_op jit(solution)/shard_map/ppermute | solution.py:30
  207.8 5.7 %collective-permute-start.2 = (bf16[128,512]{1,0:T(8,128)(2,1)S(1)}, bf16[128,512]{1,0:T(8,128)(2,1)}, u32[]{:S(2)}, u32[]{:S(2)}) collective-permute-start(bf16[128,512]{1,0:T(8,128)(2,1)S(1)} %scatter_custom_fusion.4), channel_id=1, source_target_pairs={{0,1},{1,2},{2,3},{3,4},{4,5},{5,6},{6,7},{7,8},{8,9},{9,10},{10,1... | collective-permute-start | bytes 393224 | tf_op jit(solution)/shard_map/ppermute | solution.py:30
  214.6 2.2 copy-start.7
  216.7 1.4 copy-start.13
  216.7 1.4 copy-start.14
  216.7 1.4 copy-start.15
  216.8 1.5 copy-start.18
Sparse Core Ops, SparseCore 0:
  198.9 287.9 all-reduce.2
